TPU v7x, 256 devices: a whole 4x4x8 slice. The times are simulated.
256 devices in a mesh: st: 16 (over y, x), tp: 16 (over z, core).
Axes of the slice: x: 4, y: 4, z: 8, core: 2. Of those that a mesh axis runs over, the one named last changes fastest.
Arguments:
- continuous: bfloat16 [512, 3, 1424], P(('st', 'tp')), may hold values from -48 to 48
- templates: bfloat16 [512, 12, 3, 400], P(('st', 'tp')), may hold values from -120 to 120
- station_list: int32 [512, 12], P(('st', 'tp')), may hold values from 0 to 511, as said below
- moveouts: int32 [512, 12], P(('st', 'tp')), may hold values from 0 to 256
Outputs:
- detection: float32 [512, 768], P(('st', 'tp'))
Inputs may be any that keep to these rules, and one draw needn't show every extreme that they name: `station_list`: A station's group is station // 32. The 12 stations of a template are distinct, and so are their indices within their groups (station % 32). The rows of one device (2 templates, aligned blocks in order) name at most 3 stations of any one group, and in every such block one group is named exactly 3 times; blocks b and b2 with b % 16 == b2 % 16 share that group.
All inputs are finite; a program needn't handle non-finite values.
Results may differ from a plain program's by a relative error of at most 0.0003.
Values may be sent and summed in bfloat16 or wider, within the bound.
No kernel may reach another device: no remote copies, remote signals or barrier semaphores. Data moves between devices by JAX's collectives and lax.ppermute only.
A program may use at most 64 MiB of HBM per device.

v0:
```python
import math
import jax
import jax.numpy as jnp
from jax import lax
from jax.sharding import PartitionSpec as P

WIN = 768
TLEN = 400
CH = 3
OUT = 1024
EPS = 1e-05


def frame_width():
    return 128


def toeplitz(vector, row_width, frame_size):
    leading = vector.shape[:-1]
    padded = jnp.concatenate(
        [vector, jnp.zeros(leading + (row_width + 1 - vector.shape[-1],), vector.dtype)], axis=-1
    )
    repeated = jnp.tile(padded, (1,) * len(leading) + (frame_size,))
    return repeated[..., : frame_size * row_width].reshape(leading + (frame_size, row_width))


def to_frames(series, frame_size, frame_count):
    target = frame_size * frame_count
    length_now = series.shape[-1]
    if length_now >= target:
        fitted = series[..., :target]
    else:
        fitted = jnp.concatenate(
            [series, jnp.zeros(series.shape[:-1] + (target - length_now,), series.dtype)], axis=-1
        )
    return fitted.reshape(series.shape[:-1] + (frame_count, frame_size))


def inverse_level(row_data):
    squares = jnp.square(row_data.astype(jnp.float32))
    running = jnp.cumsum(squares, axis=-1)
    running = jnp.concatenate([jnp.zeros(running.shape[:-1] + (1,), jnp.float32), running], axis=-1)
    energy = running[..., TLEN : TLEN + OUT] - running[..., :OUT]
    return lax.rsqrt(energy / TLEN + EPS)


def correlate(templates, row_data, inverse, shifts):
    frame_size = frame_width()
    blocks = OUT // frame_size
    step_count = (TLEN + 2 * frame_size - 2) // frame_size
    frames = to_frames(row_data, frame_size, blocks + step_count - 1)
    bands = toeplitz(templates, step_count * frame_size, frame_size)
    running = jnp.zeros(templates.shape[:-1] + (blocks, frame_size), jnp.float32)
    for step_index in range(step_count):
        running = running + jnp.einsum(
            "ncbp,ncip->ncbi",
            frames[:, :, step_index : step_index + blocks],
            bands[..., step_index * frame_size : (step_index + 1) * frame_size],
            preferred_element_type=jnp.float32,
        )
    raw_sums = running.reshape(templates.shape[:-1] + (OUT,))
    template_values = templates.astype(jnp.float32)
    template_inverse = lax.rsqrt(jnp.mean(template_values * template_values, axis=-1) + EPS)
    scaled = raw_sums * inverse * (template_inverse / TLEN)[..., None]
    summed = jnp.sum(scaled, axis=1)
    return jax.vmap(lambda series, start_at: lax.dynamic_slice_in_dim(series, start_at, WIN))(
        summed, shifts
    )


def in_blocks(worker, arrays, item_count):
    block_size = math.gcd(item_count, 32)
    grouped = jax.tree.map(
        lambda member: member.reshape((item_count // block_size, block_size) + member.shape[1:]),
        arrays,
    )
    result = lax.map(worker, grouped)
    return result.reshape((item_count,) + result.shape[2:])


def shards(continuous, templates, station_list, moveouts):
    group_count = lax.axis_size("st")
    template_count = templates.shape[0]
    list_size = templates.shape[1]
    group_size = continuous.shape[0] * lax.axis_size("tp")
    entries = template_count * list_size
    capacity = 2 * entries // group_count
    slots_total = group_count * capacity
    flat_list = station_list.reshape(entries)
    owners = flat_list // group_size
    within = flat_list - owners * group_size
    member = (owners[:, None] == jnp.arange(group_count, dtype=jnp.int32)[None, :]).astype(
        jnp.int32
    )
    earlier = jnp.cumsum(member, axis=0) - member
    position = jnp.sum(earlier * member, axis=1)
    slot_index = owners * capacity + position
    flat_shift = moveouts.reshape(entries)
    flat_templates = templates.reshape(entries, CH, TLEN)
    group_rows = lax.all_gather(continuous, "tp", axis=0, tiled=True)
    local_scale = inverse_level(continuous)
    group_scale = lax.all_gather(local_scale, "tp", axis=0, tiled=True)
    slot_templates = (
        jnp.zeros((slots_total, CH, TLEN), jnp.bfloat16)
        .at[slot_index]
        .set(flat_templates)
        .reshape(group_count, capacity, CH, TLEN)
    )
    slot_station = (
        jnp.zeros((slots_total,), jnp.int32)
        .at[slot_index]
        .set(within)
        .reshape(group_count, capacity)
    )
    slot_shift = (
        jnp.zeros((slots_total,), jnp.int32)
        .at[slot_index]
        .set(flat_shift)
        .reshape(group_count, capacity)
    )
    template_rows = jnp.arange(entries, dtype=jnp.int32) // list_size
    slot_row = (
        jnp.full((slots_total,), -1, jnp.int32)
        .at[slot_index]
        .set(template_rows)
        .reshape(group_count, capacity)
    )
    pieces = (
        lax.all_to_all(slot_templates, "st", split_axis=0, concat_axis=0, tiled=True),
        lax.all_to_all(slot_station, "st", split_axis=0, concat_axis=0, tiled=True),
        lax.all_to_all(slot_shift, "st", split_axis=0, concat_axis=0, tiled=True),
        lax.all_to_all(slot_row, "st", split_axis=0, concat_axis=0, tiled=True),
    )
    given_items = pieces[1].shape[1]
    item_total = group_count * given_items
    stations = pieces[1].reshape(item_total)

    def block_work(block_parts):
        picked = group_rows[block_parts[1]]
        scales = group_scale[block_parts[1]]
        return correlate(block_parts[0], picked, scales, block_parts[2])

    aligned = in_blocks(
        block_work,
        (pieces[0].reshape(item_total, CH, TLEN), stations, pieces[2].reshape(item_total)),
        item_total,
    )
    aligned = aligned.reshape(group_count, given_items, WIN)
    outcome = lax.all_to_all(aligned, "st", split_axis=0, concat_axis=0, tiled=True)
    returned = outcome.reshape(slots_total, WIN)
    detection = jnp.sum(returned[slot_index].reshape(template_count, list_size, WIN), axis=1)
    return detection


def solution(mesh):
    placed = (
        P(("st", "tp"), None, None),
        P(("st", "tp"), None, None, None),
        P(("st", "tp"), None),
        P(("st", "tp"), None),
    )
    return jax.shard_map(
        shards, mesh=mesh, in_specs=placed, out_specs=P(("st", "tp"), None), check_vma=False
    )
```

profile of v0, /device:TPU:1, one launch (start us, length us, event | category | flops | bytes accessed | tf_op | source)
XLA Modules:
  0.0 315.8 jit_solution(9241197503857095357)
XLA Ops:
  3.2 7.6 %all-to-all-start = ((s32[16,1,3]{2,1,0:T(1,128)}), s32[16,1,3]{2,1,0:T(1,128)S(1)}, u32[]{:S(2)}, u32[]{:S(2)}) async-start(s32[16,1,3]{2,1,0:T(1,128)} %bitcast.7), calls=%async_computation | async-start | bytes 16384 | tf_op jit(solution)/shard_map/all_to_all | solution.py:130
  13.8 1.7 reduce-window.6
  16.6 22.2 %all_gather.7 = f32[32,3,1024]{2,1,0:T(4,128)S(1)} all-gather(f32[2,3,1024]{2,1,0:T(4,128)S(1)} %copy.76), channel_id=1, replica_groups=mesh['st'=16,'tp'=16] {'tp'}, dimensions={0}, use_global_device_ids=true | all-gather | bytes 417792 | tf_op jit(solution)/shard_map/all_gather | solution.py:102
  39.6 6.9 %all-to-all-start.2 = ((s32[16,1,3]{2,1,0:T(1,128)}), s32[16,1,3]{2,1,0:T(1,128)S(1)}, u32[]{:S(2)}, u32[]{:S(2)}) async-start(s32[16,1,3]{2,1,0:T(1,128)} %bitcast.11), calls=%async_computation.2 | async-start | bytes 16384 | tf_op jit(solution)/shard_map/all_to_all | solution.py:131
  46.6 1.5 scatter_fusion
  48.9 3.9 %all-to-all-done.2 = s32[16,1,3]{2,1,0:T(1,128)S(1)} async-done(((s32[16,1,3]{2,1,0:T(1,128)}), s32[16,1,3]{2,1,0:T(1,128)S(1)}, u32[]{:S(2)}, u32[]{:S(2)}) %all-to-all-start.2) | async-done | bytes 224 | tf_op jit(solution)/shard_map/all_to_all | solution.py:131
  52.8 3.5 %all-to-all-start.1 = ((bf16[16,3,3,400]{3,1,2,0:T(4,128)(2,1)}), bf16[16,3,3,400]{3,1,2,0:T(4,128)(2,1)S(1)}, u32[]{:S(2)}, u32[]{:S(2)}) async-start(bf16[16,3,3,400]{3,1,2,0:T(4,128)(2,1)} %copy.70), calls=%async_computation.1 | async-start | bytes 393216 | tf_op jit(solution)/shard_map/all_to_all | solution.py:129
  56.3 16.9 %all_gather.6 = bf16[32,3,1424]{2,1,0:T(4,128)(2,1)S(1)} all-gather(bf16[2,3,1424]{2,1,0:T(4,128)(2,1)S(1)} %copy.67), channel_id=1, replica_groups=mesh['st'=16,'tp'=16] {'tp'}, dimensions={0}, use_global_device_ids=true | all-gather | bytes 290496 | tf_op jit(solution)/shard_map/all_gather | solution.py:100
  75.9 222.4 %while.13 = (s32[]{:T(128)}, f32[3,16,768]{2,1,0:T(8,128)}, s32[3,16]{1,0:T(4,128)S(1)}, bf16[32,3,1424]{2,1,0:T(4,128)(2,1)S(1)}, bf16[3,16,3,400]{3,1,0,2:T(8,...) while((s32[]{:T(128)}, f32[3,16,768]{2,1,0:T(8,128)}, ...), condition=%wide.region_10.11_spmd, body=%wide.region_7.10_spmd.sunk | while | flops 63301088 | bytes 91004616 | solution.py:77
  77.8 4.3 %tile.11 = bf16[16,3,128,641]{3,2,0,1:T(8,128)(2,1)} broadcast(bf16[16,3,641]{2,0,1:T(8,128)(2,1)S(1)} %concatenate.21), dimensions={0,1,3} | broadcast | bytes 7938144 | tf_op jit(solution)/shard_map/while/body/eval_jaxpr/tile | solution.py:23
  82.1 14.9 %tile.12 = bf16[16,3,82048]{2,0,1:T(8,128)(2,1)} reshape(bf16[16,3,128,641]{3,2,0,1:T(8,128)(2,1)} %tile.11) | data formatting | bytes 15753216 | tf_op jit(solution)/shard_map/while/body/eval_jaxpr/tile | solution.py:23
  97.0 3.2 %slice-done = bf16[16,3,81920]{2,0,1:T(8,128)(2,1)S(1)} async-done(((bf16[16,3,82048]{2,0,1:T(8,128)(2,1)}), bf16[16,3,81920]{2,0,1:T(8,128)(2,1)S(1)}, s32[]{:S(2)}) %slice-start) | async-done | bytes 7864344 | tf_op jit(solution)/shard_map/while/body/eval_jaxpr/slice | solution.py:24
  100.2 4.6 %copy.136 = bf16[6,8,128,640]{3,2,1,0:T(8,128)(2,1)} copy(bf16[6,8,128,640]{3,1,2,0:T(8,128)(2,1)S(1)} %bitcast.72) | data formatting | bytes 15728640 | tf_op jit(solution)/shard_map/while
  104.8 3.7 %fusion.78 = (bf16[16,3,128,128]{3,2,0,1:T(8,128)(2,1)S(1)}, bf16[16,3,128,128]{3,2,0,1:T(8,128)(2,1)S(1)}, bf16[16,3,128,128]{3,2,0,1:T(8,128)(2,1)S(1)}, bf16[...) fusion(bf16[16,3,128,640]{3,2,0,1:T(8,128)(2,1)} %bitcast.73), kind=kLoop, calls=%fused_computation.70.clone.1 | loop fusion | bytes 15728640 | tf_op jit(solution)/shard_map/while/body/eval_jaxpr/slice | solution.py:58
  114.1 35.3 %while.14 = (s32[]{:T(128)}, f32[16,1024]{1,0:T(8,128)S(1)}, s32[16,2]{0,1:T(2,128)S(1)}, f32[16,768]{1,0:T(8,128)S(1)}, s32[]{:T(128)}, /*index=5*/s32[]{:T(128)}) while((s32[]{:T(128)}, f32[16,1024]{1,0:T(8,128)S(1)}, s32[16,2]{0,1:T(2,128)S(1)}, f32[16,768]{1,0:T(8,128)S(1)}, s32[]{:T(128)}, /*index=5*/s32[]{:T(128)}) %tuple.55), condition=%wide.while_cond, body=%wide.while_body.sunk | while | flops 2 | bytes 12401 | solution.py:66
  114.8 1.5 dynamic-slice.7
  117.0 1.5 dynamic-slice.7
  119.2 1.5 dynamic-slice.7
  121.4 1.5 dynamic-slice.7
  123.6 1.5 dynamic-slice.7
  125.9 1.5 dynamic-slice.7
  128.1 1.5 dynamic-slice.7
  130.3 1.5 dynamic-slice.7
  132.5 1.5 dynamic-slice.7
  134.7 1.5 dynamic-slice.7
  136.9 1.5 dynamic-slice.7
  139.1 1.5 dynamic-slice.7
  141.3 1.5 dynamic-slice.7
  152.0 4.3 %tile.11 = bf16[16,3,128,641]{3,2,0,1:T(8,128)(2,1)} broadcast(bf16[16,3,641]{2,0,1:T(8,128)(2,1)S(1)} %concatenate.21), dimensions={0,1,3} | broadcast | bytes 7938144 | tf_op jit(solution)/shard_map/while/body/eval_jaxpr/tile | solution.py:23
  156.2 14.9 %tile.12 = bf16[16,3,82048]{2,0,1:T(8,128)(2,1)} reshape(bf16[16,3,128,641]{3,2,0,1:T(8,128)(2,1)} %tile.11) | data formatting | bytes 15753216 | tf_op jit(solution)/shard_map/while/body/eval_jaxpr/tile | solution.py:23
  171.1 3.2 %slice-done = bf16[16,3,81920]{2,0,1:T(8,128)(2,1)S(1)} async-done(((bf16[16,3,82048]{2,0,1:T(8,128)(2,1)}), bf16[16,3,81920]{2,0,1:T(8,128)(2,1)S(1)}, s32[]{:S(2)}) %slice-start) | async-done | bytes 7864344 | tf_op jit(solution)/shard_map/while/body/eval_jaxpr/slice | solution.py:24
  174.4 4.6 %copy.136 = bf16[6,8,128,640]{3,2,1,0:T(8,128)(2,1)} copy(bf16[6,8,128,640]{3,1,2,0:T(8,128)(2,1)S(1)} %bitcast.72) | data formatting | bytes 15728640 | tf_op jit(solution)/shard_map/while
  178.9 3.7 %fusion.78 = (bf16[16,3,128,128]{3,2,0,1:T(8,128)(2,1)S(1)}, bf16[16,3,128,128]{3,2,0,1:T(8,128)(2,1)S(1)}, bf16[16,3,128,128]{3,2,0,1:T(8,128)(2,1)S(1)}, bf16[...) fusion(bf16[16,3,128,640]{3,2,0,1:T(8,128)(2,1)} %bitcast.73), kind=kLoop, calls=%fused_computation.70.clone.1 | loop fusion | bytes 15728640 | tf_op jit(solution)/shard_map/while/body/eval_jaxpr/slice | solution.py:58
  188.3 35.3 %while.14 = (s32[]{:T(128)}, f32[16,1024]{1,0:T(8,128)S(1)}, s32[16,2]{0,1:T(2,128)S(1)}, f32[16,768]{1,0:T(8,128)S(1)}, s32[]{:T(128)}, /*index=5*/s32[]{:T(128)}) while((s32[]{:T(128)}, f32[16,1024]{1,0:T(8,128)S(1)}, s32[16,2]{0,1:T(2,128)S(1)}, f32[16,768]{1,0:T(8,128)S(1)}, s32[]{:T(128)}, /*index=5*/s32[]{:T(128)}) %tuple.55), condition=%wide.while_cond, body=%wide.while_body.sunk | while | flops 2 | bytes 12401 | solution.py:66
  197.8 1.5 dynamic-slice.7
  208.8 1.5 dynamic-slice.7
  226.1 4.3 %tile.11 = bf16[16,3,128,641]{3,2,0,1:T(8,128)(2,1)} broadcast(bf16[16,3,641]{2,0,1:T(8,128)(2,1)S(1)} %concatenate.21), dimensions={0,1,3} | broadcast | bytes 7938144 | tf_op jit(solution)/shard_map/while/body/eval_jaxpr/tile | solution.py:23
  230.4 14.9 %tile.12 = bf16[16,3,82048]{2,0,1:T(8,128)(2,1)} reshape(bf16[16,3,128,641]{3,2,0,1:T(8,128)(2,1)} %tile.11) | data formatting | bytes 15753216 | tf_op jit(solution)/shard_map/while/body/eval_jaxpr/tile | solution.py:23
  245.3 3.2 %slice-done = bf16[16,3,81920]{2,0,1:T(8,128)(2,1)S(1)} async-done(((bf16[16,3,82048]{2,0,1:T(8,128)(2,1)}), bf16[16,3,81920]{2,0,1:T(8,128)(2,1)S(1)}, s32[]{:S(2)}) %slice-start) | async-done | bytes 7864344 | tf_op jit(solution)/shard_map/while/body/eval_jaxpr/slice | solution.py:24
  248.5 4.6 %copy.136 = bf16[6,8,128,640]{3,2,1,0:T(8,128)(2,1)} copy(bf16[6,8,128,640]{3,1,2,0:T(8,128)(2,1)S(1)} %bitcast.72) | data formatting | bytes 15728640 | tf_op jit(solution)/shard_map/while
  253.1 3.7 %fusion.78 = (bf16[16,3,128,128]{3,2,0,1:T(8,128)(2,1)S(1)}, bf16[16,3,128,128]{3,2,0,1:T(8,128)(2,1)S(1)}, bf16[16,3,128,128]{3,2,0,1:T(8,128)(2,1)S(1)}, bf16[...) fusion(bf16[16,3,128,640]{3,2,0,1:T(8,128)(2,1)} %bitcast.73), kind=kLoop, calls=%fused_computation.70.clone.1 | loop fusion | bytes 15728640 | tf_op jit(solution)/shard_map/while/body/eval_jaxpr/slice | solution.py:58
  262.4 35.3 %while.14 = (s32[]{:T(128)}, f32[16,1024]{1,0:T(8,128)S(1)}, s32[16,2]{0,1:T(2,128)S(1)}, f32[16,768]{1,0:T(8,128)S(1)}, s32[]{:T(128)}, /*index=5*/s32[]{:T(128)}) while((s32[]{:T(128)}, f32[16,1024]{1,0:T(8,128)S(1)}, s32[16,2]{0,1:T(2,128)S(1)}, f32[16,768]{1,0:T(8,128)S(1)}, s32[]{:T(128)}, /*index=5*/s32[]{:T(128)}) %tuple.55), condition=%wide.while_cond, body=%wide.while_body.sunk | while | flops 2 | bytes 12401 | solution.py:66
  263.1 1.5 dynamic-slice.7
  274.1 1.5 dynamic-slice.7
  294.0 1.5 dynamic-slice.7
  298.4 1.6 reshape_reshape.15
  300.0 6.9 %all-to-all-start.3 = ((f32[16,3,768]{2,1,0:T(4,128)}), f32[16,3,768]{2,1,0:T(4,128)S(1)}, u32[]{:S(2)}, u32[]{:S(2)}) async-start(f32[16,3,768]{2,1,0:T(4,128)} %reshape_reshape.15), calls=%async_computation.3 | async-start | bytes 393216 | tf_op jit(solution)/shard_map/all_to_all | solution.py:149
  306.9 7.6 %all-to-all-done.3 = f32[16,3,768]{2,1,0:T(4,128)S(1)} async-done(((f32[16,3,768]{2,1,0:T(4,128)}), f32[16,3,768]{2,1,0:T(4,128)S(1)}, u32[]{:S(2)}, u32[]{:S(2)}) %all-to-all-start.3) | async-done | bytes 147488 | tf_op jit(solution)/shard_map/all_to_all | solution.py:149
  (290 shorter events, 115.6 us)
Async XLA Ops:
  0.0 39.5 %copy-start = (bf16[2,12,3,400]{3,0,2,1:T(2,128)(2,1)S(1)}, bf16[2,12,3,400]{3,0,2,1:T(2,128)(2,1)}, u32[]{:S(2)}) copy-start(bf16[2,12,3,400]{3,0,2,1:T(2,128)(2,1)} %param.7) | copy-start | bytes 172804
  3.2 36.3 %all-to-all-start = ((s32[16,1,3]{2,1,0:T(1,128)}), s32[16,1,3]{2,1,0:T(1,128)S(1)}, u32[]{:S(2)}, u32[]{:S(2)}) async-start(s32[16,1,3]{2,1,0:T(1,128)} %bitcast.7), calls=%async_computation | async-start | bytes 16384 | tf_op jit(solution)/shard_map/all_to_all | solution.py:130
  39.6 13.2 %all-to-all-start.2 = ((s32[16,1,3]{2,1,0:T(1,128)}), s32[16,1,3]{2,1,0:T(1,128)S(1)}, u32[]{:S(2)}, u32[]{:S(2)}) async-start(s32[16,1,3]{2,1,0:T(1,128)} %bitcast.11), calls=%async_computation.2 | async-start | bytes 16384 | tf_op jit(solution)/shard_map/all_to_all | solution.py:131
  52.8 22.3 %all-to-all-start.1 = ((bf16[16,3,3,400]{3,1,2,0:T(4,128)(2,1)}), bf16[16,3,3,400]{3,1,2,0:T(4,128)(2,1)S(1)}, u32[]{:S(2)}, u32[]{:S(2)}) async-start(bf16[16,3,3,400]{3,1,2,0:T(4,128)(2,1)} %copy.70), calls=%async_computation.1 | async-start | bytes 393216 | tf_op jit(solution)/shard_map/all_to_all | solution.py:129
  97.0 3.2 %slice-start = ((bf16[16,3,82048]{2,0,1:T(8,128)(2,1)}), bf16[16,3,81920]{2,0,1:T(8,128)(2,1)S(1)}, s32[]{:S(2)}) async-start(bf16[16,3,82048]{2,0,1:T(8,128)(2,1)} %tile.12), calls=%async_computation.4 | async-start | bytes 15728640 | tf_op jit(solution)/shard_map/while/body/eval_jaxpr/slice | solution.py:24
  171.1 3.2 %slice-start = ((bf16[16,3,82048]{2,0,1:T(8,128)(2,1)}), bf16[16,3,81920]{2,0,1:T(8,128)(2,1)S(1)}, s32[]{:S(2)}) async-start(bf16[16,3,82048]{2,0,1:T(8,128)(2,1)} %tile.12), calls=%async_computation.4 | async-start | bytes 15728640 | tf_op jit(solution)/shard_map/while/body/eval_jaxpr/slice | solution.py:24
  245.3 3.2 %slice-start = ((bf16[16,3,82048]{2,0,1:T(8,128)(2,1)}), bf16[16,3,81920]{2,0,1:T(8,128)(2,1)S(1)}, s32[]{:S(2)}) async-start(bf16[16,3,82048]{2,0,1:T(8,128)(2,1)} %tile.12), calls=%async_computation.4 | async-start | bytes 15728640 | tf_op jit(solution)/shard_map/while/body/eval_jaxpr/slice | solution.py:24
  300.0 14.5 %all-to-all-start.3 = ((f32[16,3,768]{2,1,0:T(4,128)}), f32[16,3,768]{2,1,0:T(4,128)S(1)}, u32[]{:S(2)}, u32[]{:S(2)}) async-start(f32[16,3,768]{2,1,0:T(4,128)} %reshape_reshape.15), calls=%async_computation.3 | async-start | bytes 393216 | tf_op jit(solution)/shard_map/all_to_all | solution.py:149
where the time goes:
time: 318 us; the launch traced here: 316 us
  local copies, waits for them, and re-layouts  217 us (68%)
  blocking collectives  39.1 us (12%)
  starting transfers between devices  24.9 us (8%)
  matrix products  13.8 us (4%)
  waiting for transfers between devices  11.5 us (4%)
  other arithmetic  8.16 us (3%)
    gather x192, local copies, waits for them, and re-layouts  105 us
    another operation x6, local copies, waits for them, and re-layouts, toeplitz(): repeated = jnp.tile(padded, (1,) * len(leading) + (frame_size,))  57.4 us
    all_gather x1, blocking collectives, shards(): group_scale = lax.all_gather(local_scale, 'tp', axis=0, tiled=True)  22.2 us
    all_gather x1, blocking collectives, shards(): group_rows = lax.all_gather(continuous, 'tp', axis=0, tiled=True)  16.9 us
    dot_general x15, matrix products, correlate(): jnp.einsum('ncbp,ncip->ncbi', frames[:, :, step_index:step_index + blocks...  13.8 us
    while x9, local copies, waits for them, and re-layouts  13.8 us
    slice x3, local copies, waits for them, and re-layouts, correlate(): bands[..., step_index * frame_size:(step_index + 1) * frame_size]  11.2 us
    slice x6, local copies, waits for them, and re-layouts, toeplitz(): repeated[..., :frame_size * row_width]  9.7 us
  transfers between devices with their start and end apart: 4, of which 2 were waited for; matrix products, arithmetic and copies ran while one was open for 3% of the time, Pallas kernels for 0%

commit v1 on v0

--- a/solution.py
+++ b/solution.py
@@ -9,6 +9,22 @@
 CH = 3
 OUT = 1024
 EPS = 1e-05
+
+
+def gather_around(x, axis, dim):
+    ways, here, step = (lax.axis_size(axis), lax.axis_index(axis), x.shape[dim])
+    lengths = [n * ways if d == dim else n for d, n in enumerate(x.shape)]
+    full = lax.dynamic_update_slice_in_dim(jnp.zeros(lengths, x.dtype), x, here * step, axis=dim)
+    going_up = going_down = x
+    for far in range(1, ways // 2 + 1):
+        going_up = lax.ppermute(going_up, axis, [(d, (d + 1) % ways) for d in range(ways)])
+        full = lax.dynamic_update_slice_in_dim(full, going_up, (here - far) % ways * step, axis=dim)
+        if 2 * far < ways:
+            going_down = lax.ppermute(going_down, axis, [(d, (d - 1) % ways) for d in range(ways)])
+            full = lax.dynamic_update_slice_in_dim(
+                full, going_down, (here + far) % ways * step, axis=dim
+            )
+    return full
 
 
 def frame_width():
@@ -97,7 +113,7 @@
     slot_index = owners * capacity + position
     flat_shift = moveouts.reshape(entries)
     flat_templates = templates.reshape(entries, CH, TLEN)
-    group_rows = lax.all_gather(continuous, "tp", axis=0, tiled=True)
+    group_rows = gather_around(continuous, "tp", 0)
     local_scale = inverse_level(continuous)
     group_scale = lax.all_gather(local_scale, "tp", axis=0, tiled=True)
     slot_templates = (

time: 318 us -> 321 us (level)
  starting transfers between devices: 24.9 us -> 47 us
  blocking collectives: 39.1 us -> 21.7 us
  local copies, waits for them, and re-layouts: 217 us -> 204 us
  waiting for transfers between devices: 11.5 us -> 20.1 us
    ppermute x0 -> x15, starting transfers between devices: none -> 23.2 us  [the longest x7 16.5 us: gather_around(): lax.ppermute(going_down, axis, [(d, (d - 1) % ways) for d in range(ways)])]
    all_gather x1 -> x0, blocking collectives: 16.9 us -> none  [shards(): group_rows = lax.all_gather(continuous, 'tp', axis=0, tiled=True)]
    gather x192, local copies, waits for them, and re-layouts: 105 us -> 92.1 us
    ppermute x0 -> x15, waiting for transfers between devices: none -> 7.82 us  [the longest x8 6.09 us: gather_around(): lax.ppermute(going_up, axis, [(d, (d + 1) % ways) for d in range(ways)])]
  transfers between devices with their start and end apart: 4 -> 19, of which waited for: 2 -> 12; matrix products, arithmetic and copies ran while one was open for 3% -> 4% of each run, Pallas kernels for 0% -> 0%
where the time goes in v1:
time: 321 us; the launch traced here: 317 us
  local copies, waits for them, and re-layouts  204 us (64%)
  starting transfers between devices  47 us (15%)
  blocking collectives  21.7 us (7%)
  waiting for transfers between devices  20.1 us (6%)
  matrix products  13.8 us (4%)
  other arithmetic  8.3 us (3%)
    gather x192, local copies, waits for them, and re-layouts  92.1 us
    another operation x6, local copies, waits for them, and re-layouts, toeplitz(): repeated = jnp.tile(padded, (1,) * len(leading) + (frame_size,))  57.4 us
    all_gather x1, blocking collectives, shards(): group_scale = lax.all_gather(local_scale, 'tp', axis=0, tiled=True)  21.7 us
    ppermute x7, starting transfers between devices, gather_around(): lax.ppermute(going_down, axis, [(d, (d - 1) % ways) for d in range(ways)])  16.5 us
    while x9, local copies, waits for them, and re-layouts  13.8 us
    dot_general x15, matrix products, correlate(): jnp.einsum('ncbp,ncip->ncbi', frames[:, :, step_index:step_index + blocks...  13.8 us
    slice x3, local copies, waits for them, and re-layouts, correlate(): bands[..., step_index * frame_size:(step_index + 1) * frame_size]  11.2 us
    slice x6, local copies, waits for them, and re-layouts, toeplitz(): repeated[..., :frame_size * row_width]  9.7 us
  transfers between devices with their start and end apart: 19, of which 12 were waited for; matrix products, arithmetic and copies ran while one was open for 4% of the time, Pallas kernels for 0%

profile of v1, /device:TPU:1, one launch (start us, length us, event | category | flops | bytes accessed | tf_op | source)
XLA Modules:
  0.0 316.6 jit_solution(2005104480942237494)
XLA Ops:
  0.9 3.0 collective-permute-start
  7.3 6.5 %all-to-all-start = ((s32[16,1,3]{2,1,0:T(1,128)}), s32[16,1,3]{2,1,0:T(1,128)S(1)}, u32[]{:S(2)}, u32[]{:S(2)}) async-start(s32[16,1,3]{2,1,0:T(1,128)} %bitcast.7), calls=%async_computation | async-start | bytes 16384 | tf_op jit(solution)/shard_map/all_to_all | solution.py:146
  14.7 1.7 reduce-window.6
  17.5 21.7 %all_gather.3 = f32[32,3,1024]{2,1,0:T(4,128)S(1)} all-gather(f32[2,3,1024]{2,1,0:T(4,128)S(1)} %copy.84), channel_id=1, replica_groups=mesh['st'=16,'tp'=16] {'tp'}, dimensions={0}, use_global_device_ids=true | all-gather | bytes 417792 | tf_op jit(solution)/shard_map/all_gather | solution.py:118
  40.8 1.5 scatter_fusion
  43.1 6.9 %all-to-all-start.2 = ((s32[16,1,3]{2,1,0:T(1,128)}), s32[16,1,3]{2,1,0:T(1,128)S(1)}, u32[]{:S(2)}, u32[]{:S(2)}) async-start(s32[16,1,3]{2,1,0:T(1,128)} %bitcast.11), calls=%async_computation.2 | async-start | bytes 16384 | tf_op jit(solution)/shard_map/all_to_all | solution.py:147
  51.3 5.1 %all-to-all-done.2 = s32[16,1,3]{2,1,0:T(1,128)S(1)} async-done(((s32[16,1,3]{2,1,0:T(1,128)}), s32[16,1,3]{2,1,0:T(1,128)S(1)}, u32[]{:S(2)}, u32[]{:S(2)}) %all-to-all-start.2) | async-done | bytes 224 | tf_op jit(solution)/shard_map/all_to_all | solution.py:147
  56.5 3.5 %all-to-all-start.1 = ((bf16[16,3,3,400]{3,1,2,0:T(4,128)(2,1)}), bf16[16,3,3,400]{3,1,2,0:T(4,128)(2,1)S(1)}, u32[]{:S(2)}, u32[]{:S(2)}) async-start(bf16[16,3,3,400]{3,1,2,0:T(4,128)(2,1)} %copy.78), calls=%async_computation.1 | async-start | bytes 393216 | tf_op jit(solution)/shard_map/all_to_all | solution.py:145
  62.9 2.0 collective-permute-start.4
  64.9 1.8 collective-permute-start.5
  68.4 3.0 collective-permute-start.7
  72.3 3.6 %collective-permute-start.9 = (bf16[2,3,1424]{2,1,0:T(4,128)(2,1)S(1)}, bf16[2,3,1424]{2,1,0:T(4,128)(2,1)S(1)}, u32[]{:S(2)}, u32[]{:S(2)}) collective-permute-start(bf16[2,3,1424]{2,1,0:T(4,128)(2,1)S(1)} %collective-permute-done.7), channel_id=1, source_target_pairs={{0,15},{1,0},{2,1},{3,2},{4,3},{5,4},{6,5},{7,6},{8,7},{9,8},{10,9... | collective-permute-start | bytes 51272 | tf_op jit(solution)/shard_map/ppermute | solution.py:23
  76.7 3.6 %collective-permute-start.11 = (bf16[2,3,1424]{2,1,0:T(4,128)(2,1)S(1)}, bf16[2,3,1424]{2,1,0:T(4,128)(2,1)S(1)}, u32[]{:S(2)}, u32[]{:S(2)}) collective-permute-start(bf16[2,3,1424]{2,1,0:T(4,128)(2,1)S(1)} %collective-permute-done.9), channel_id=1, source_target_pairs={{0,15},{1,0},{2,1},{3,2},{4,3},{5,4},{6,5},{7,6},{8,7},{9,8},{10,9... | collective-permute-start | bytes 51272 | tf_op jit(solution)/shard_map/ppermute | solution.py:23
  81.2 3.6 %collective-permute-start.13 = (bf16[2,3,1424]{2,1,0:T(4,128)(2,1)S(1)}, bf16[2,3,1424]{2,1,0:T(4,128)(2,1)S(1)}, u32[]{:S(2)}, u32[]{:S(2)}) collective-permute-start(bf16[2,3,1424]{2,1,0:T(4,128)(2,1)S(1)} %collective-permute-done.11), channel_id=1, source_target_pairs={{0,15},{1,0},{2,1},{3,2},{4,3},{5,4},{6,5},{7,6},{8,7},{9,8},{10,9... | collective-permute-start | bytes 51272 | tf_op jit(solution)/shard_map/ppermute | solution.py:23
  85.8 3.9 %collective-permute-done.14 = bf16[2,3,1424]{2,1,0:T(4,128)(2,1)S(1)} collective-permute-done((bf16[2,3,1424]{2,1,0:T(4,128)(2,1)S(1)}, bf16[2,3,1424]{2,1,0:T(4,128)(2,1)S(1)}, u32[]{:S(2)}, u32[]{:S(2)}) %collective-permute-start.14) | collective-permute-done | bytes 17120 | tf_op jit(solution)/shard_map/ppermute | solution.py:20
  89.7 209.9 %while.13 = (s32[]{:T(128)}, f32[3,16,768]{2,1,0:T(8,128)}, s32[3,16]{1,0:T(4,128)S(1)}, bf16[32,3,1424]{2,1,0:T(4,128)(2,1)S(1)}, bf16[3,16,3,400]{3,1,0,2:T(8,...) while((s32[]{:T(128)}, f32[3,16,768]{2,1,0:T(8,128)}, ...), condition=%wide.region_10.11_spmd, body=%wide.region_7.10_spmd.sunk | while | flops 63301088 | bytes 91004616 | solution.py:93
  91.6 4.3 %tile.11 = bf16[16,3,128,641]{3,2,0,1:T(8,128)(2,1)} broadcast(bf16[16,3,641]{2,0,1:T(8,128)(2,1)S(1)} %concatenate.21), dimensions={0,1,3} | broadcast | bytes 7938144 | tf_op jit(solution)/shard_map/while/body/eval_jaxpr/tile | solution.py:39
  95.9 14.9 %tile.12 = bf16[16,3,82048]{2,0,1:T(8,128)(2,1)} reshape(bf16[16,3,128,641]{3,2,0,1:T(8,128)(2,1)} %tile.11) | data formatting | bytes 15753216 | tf_op jit(solution)/shard_map/while/body/eval_jaxpr/tile | solution.py:39
  110.8 3.2 %slice-done = bf16[16,3,81920]{2,0,1:T(8,128)(2,1)S(1)} async-done(((bf16[16,3,82048]{2,0,1:T(8,128)(2,1)}), bf16[16,3,81920]{2,0,1:T(8,128)(2,1)S(1)}, s32[]{:S(2)}) %slice-start) | async-done | bytes 7864344 | tf_op jit(solution)/shard_map/while/body/eval_jaxpr/slice | solution.py:40
  114.0 4.6 %copy.146 = bf16[6,8,128,640]{3,2,1,0:T(8,128)(2,1)} copy(bf16[6,8,128,640]{3,1,2,0:T(8,128)(2,1)S(1)} %bitcast.72) | data formatting | bytes 15728640 | tf_op jit(solution)/shard_map/while
  118.6 3.7 %fusion.79 = (bf16[16,3,128,128]{3,2,0,1:T(8,128)(2,1)S(1)}, bf16[16,3,128,128]{3,2,0,1:T(8,128)(2,1)S(1)}, bf16[16,3,128,128]{3,2,0,1:T(8,128)(2,1)S(1)}, bf16[...) fusion(bf16[16,3,128,640]{3,2,0,1:T(8,128)(2,1)} %bitcast.73), kind=kLoop, calls=%fused_computation.86.clone.1 | loop fusion | bytes 15728640 | tf_op jit(solution)/shard_map/while/body/eval_jaxpr/slice | solution.py:74
  127.9 31.1 %while.14 = (s32[]{:T(128)}, f32[16,1024]{1,0:T(8,128)S(1)}, s32[16,2]{0,1:T(2,128)S(1)}, f32[16,768]{1,0:T(8,128)S(1)}, s32[]{:T(128)}, /*index=5*/s32[]{:T(128)}) while((s32[]{:T(128)}, f32[16,1024]{1,0:T(8,128)S(1)}, s32[16,2]{0,1:T(2,128)S(1)}, f32[16,768]{1,0:T(8,128)S(1)}, s32[]{:T(128)}, /*index=5*/s32[]{:T(128)}) %tuple.56), condition=%wide.while_cond, body=%wide.while_body.sunk | while | flops 2 | bytes 12401 | solution.py:82
  128.6 1.3 dynamic-slice.7
  130.5 1.3 dynamic-slice.7
  132.4 1.3 dynamic-slice.7
  134.4 1.3 dynamic-slice.7
  136.3 1.3 dynamic-slice.7
  138.3 1.3 dynamic-slice.7
  140.2 1.3 dynamic-slice.7
  142.2 1.3 dynamic-slice.7
  146.0 1.3 dynamic-slice.7
  148.0 1.3 dynamic-slice.7
  149.9 1.3 dynamic-slice.7
  161.6 4.3 %tile.11 = bf16[16,3,128,641]{3,2,0,1:T(8,128)(2,1)} broadcast(bf16[16,3,641]{2,0,1:T(8,128)(2,1)S(1)} %concatenate.21), dimensions={0,1,3} | broadcast | bytes 7938144 | tf_op jit(solution)/shard_map/while/body/eval_jaxpr/tile | solution.py:39
  165.8 14.9 %tile.12 = bf16[16,3,82048]{2,0,1:T(8,128)(2,1)} reshape(bf16[16,3,128,641]{3,2,0,1:T(8,128)(2,1)} %tile.11) | data formatting | bytes 15753216 | tf_op jit(solution)/shard_map/while/body/eval_jaxpr/tile | solution.py:39
  180.7 3.2 %slice-done = bf16[16,3,81920]{2,0,1:T(8,128)(2,1)S(1)} async-done(((bf16[16,3,82048]{2,0,1:T(8,128)(2,1)}), bf16[16,3,81920]{2,0,1:T(8,128)(2,1)S(1)}, s32[]{:S(2)}) %slice-start) | async-done | bytes 7864344 | tf_op jit(solution)/shard_map/while/body/eval_jaxpr/slice | solution.py:40
  184.0 4.6 %copy.146 = bf16[6,8,128,640]{3,2,1,0:T(8,128)(2,1)} copy(bf16[6,8,128,640]{3,1,2,0:T(8,128)(2,1)S(1)} %bitcast.72) | data formatting | bytes 15728640 | tf_op jit(solution)/shard_map/while
  188.5 3.7 %fusion.79 = (bf16[16,3,128,128]{3,2,0,1:T(8,128)(2,1)S(1)}, bf16[16,3,128,128]{3,2,0,1:T(8,128)(2,1)S(1)}, bf16[16,3,128,128]{3,2,0,1:T(8,128)(2,1)S(1)}, bf16[...) fusion(bf16[16,3,128,640]{3,2,0,1:T(8,128)(2,1)} %bitcast.73), kind=kLoop, calls=%fused_computation.86.clone.1 | loop fusion | bytes 15728640 | tf_op jit(solution)/shard_map/while/body/eval_jaxpr/slice | solution.py:74
  197.9 31.1 %while.14 = (s32[]{:T(128)}, f32[16,1024]{1,0:T(8,128)S(1)}, s32[16,2]{0,1:T(2,128)S(1)}, f32[16,768]{1,0:T(8,128)S(1)}, s32[]{:T(128)}, /*index=5*/s32[]{:T(128)}) while((s32[]{:T(128)}, f32[16,1024]{1,0:T(8,128)S(1)}, s32[16,2]{0,1:T(2,128)S(1)}, f32[16,768]{1,0:T(8,128)S(1)}, s32[]{:T(128)}, /*index=5*/s32[]{:T(128)}) %tuple.56), condition=%wide.while_cond, body=%wide.while_body.sunk | while | flops 2 | bytes 12401 | solution.py:82
  231.5 4.3 %tile.11 = bf16[16,3,128,641]{3,2,0,1:T(8,128)(2,1)} broadcast(bf16[16,3,641]{2,0,1:T(8,128)(2,1)S(1)} %concatenate.21), dimensions={0,1,3} | broadcast | bytes 7938144 | tf_op jit(solution)/shard_map/while/body/eval_jaxpr/tile | solution.py:39
  235.8 14.9 %tile.12 = bf16[16,3,82048]{2,0,1:T(8,128)(2,1)} reshape(bf16[16,3,128,641]{3,2,0,1:T(8,128)(2,1)} %tile.11) | data formatting | bytes 15753216 | tf_op jit(solution)/shard_map/while/body/eval_jaxpr/tile | solution.py:39
  250.7 3.2 %slice-done = bf16[16,3,81920]{2,0,1:T(8,128)(2,1)S(1)} async-done(((bf16[16,3,82048]{2,0,1:T(8,128)(2,1)}), bf16[16,3,81920]{2,0,1:T(8,128)(2,1)S(1)}, s32[]{:S(2)}) %slice-start) | async-done | bytes 7864344 | tf_op jit(solution)/shard_map/while/body/eval_jaxpr/slice | solution.py:40
  253.9 4.6 %copy.146 = bf16[6,8,128,640]{3,2,1,0:T(8,128)(2,1)} copy(bf16[6,8,128,640]{3,1,2,0:T(8,128)(2,1)S(1)} %bitcast.72) | data formatting | bytes 15728640 | tf_op jit(solution)/shard_map/while
  258.5 3.7 %fusion.79 = (bf16[16,3,128,128]{3,2,0,1:T(8,128)(2,1)S(1)}, bf16[16,3,128,128]{3,2,0,1:T(8,128)(2,1)S(1)}, bf16[16,3,128,128]{3,2,0,1:T(8,128)(2,1)S(1)}, bf16[...) fusion(bf16[16,3,128,640]{3,2,0,1:T(8,128)(2,1)} %bitcast.73), kind=kLoop, calls=%fused_computation.86.clone.1 | loop fusion | bytes 15728640 | tf_op jit(solution)/shard_map/while/body/eval_jaxpr/slice | solution.py:74
  267.8 31.1 %while.14 = (s32[]{:T(128)}, f32[16,1024]{1,0:T(8,128)S(1)}, s32[16,2]{0,1:T(2,128)S(1)}, f32[16,768]{1,0:T(8,128)S(1)}, s32[]{:T(128)}, /*index=5*/s32[]{:T(128)}) while((s32[]{:T(128)}, f32[16,1024]{1,0:T(8,128)S(1)}, s32[16,2]{0,1:T(2,128)S(1)}, f32[16,768]{1,0:T(8,128)S(1)}, s32[]{:T(128)}, /*index=5*/s32[]{:T(128)}) %tuple.56), condition=%wide.while_cond, body=%wide.while_body.sunk | while | flops 2 | bytes 12401 | solution.py:82
  299.6 1.6 reshape_reshape.15
  301.2 6.9 %all-to-all-start.3 = ((f32[16,3,768]{2,1,0:T(4,128)}), f32[16,3,768]{2,1,0:T(4,128)S(1)}, u32[]{:S(2)}, u32[]{:S(2)}) async-start(f32[16,3,768]{2,1,0:T(4,128)} %reshape_reshape.15), calls=%async_computation.3 | async-start | bytes 393216 | tf_op jit(solution)/shard_map/all_to_all | solution.py:165
  308.1 7.2 %all-to-all-done.3 = f32[16,3,768]{2,1,0:T(4,128)S(1)} async-done(((f32[16,3,768]{2,1,0:T(4,128)}), f32[16,3,768]{2,1,0:T(4,128)S(1)}, u32[]{:S(2)}, u32[]{:S(2)}) %all-to-all-start.3) | async-done | bytes 147488 | tf_op jit(solution)/shard_map/all_to_all | solution.py:165
  (337 shorter events, 121.6 us)
Async XLA Ops:
  0.0 39.3 %copy-start.1 = (s32[2,12]{1,0:T(2,128)S(1)}, s32[2,12]{1,0:T(2,128)}, u32[]{:S(2)}) copy-start(s32[2,12]{1,0:T(2,128)} %param.9) | copy-start | bytes 292
  0.0 40.7 %copy-start = (bf16[2,12,3,400]{3,0,2,1:T(2,128)(2,1)S(1)}, bf16[2,12,3,400]{3,0,2,1:T(2,128)(2,1)}, u32[]{:S(2)}) copy-start(bf16[2,12,3,400]{3,0,2,1:T(2,128)(2,1)} %param.7) | copy-start | bytes 172804
  0.9 59.9 %collective-permute-start = (bf16[2,3,1424]{2,1,0:T(4,128)(2,1)S(1)}, bf16[2,3,1424]{2,1,0:T(4,128)(2,1)S(1)}, u32[]{:S(2)}, u32[]{:S(2)}) collective-permute-start(bf16[2,3,1424]{2,1,0:T(4,128)(2,1)S(1)} %get-tuple-element.105), channel_id=1, source_target_pairs={{0,1},{1,2},{2,3},{3,4},{4,5},{5,6},{6,7},{7,8},{8,9},{9,10},{10,1... | collective-permute-start | bytes 51272 | tf_op jit(solution)/shard_map/ppermute | solution.py:20
  3.9 57.7 %collective-permute-start.1 = (bf16[2,3,1424]{2,1,0:T(4,128)(2,1)S(1)}, bf16[2,3,1424]{2,1,0:T(4,128)(2,1)S(1)}, u32[]{:S(2)}, u32[]{:S(2)}) collective-permute-start(bf16[2,3,1424]{2,1,0:T(4,128)(2,1)S(1)} %get-tuple-element.105), channel_id=1, source_target_pairs={{0,15},{1,0},{2,1},{3,2},{4,3},{5,4},{6,5},{7,6},{8,7},{9,8},{10,9... | collective-permute-start | bytes 51272 | tf_op jit(solution)/shard_map/ppermute | solution.py:23
  7.3 35.8 %all-to-all-start = ((s32[16,1,3]{2,1,0:T(1,128)}), s32[16,1,3]{2,1,0:T(1,128)S(1)}, u32[]{:S(2)}, u32[]{:S(2)}) async-start(s32[16,1,3]{2,1,0:T(1,128)} %bitcast.7), calls=%async_computation | async-start | bytes 16384 | tf_op jit(solution)/shard_map/all_to_all | solution.py:146
  43.1 13.4 %all-to-all-start.2 = ((s32[16,1,3]{2,1,0:T(1,128)}), s32[16,1,3]{2,1,0:T(1,128)S(1)}, u32[]{:S(2)}, u32[]{:S(2)}) async-start(s32[16,1,3]{2,1,0:T(1,128)} %bitcast.11), calls=%async_computation.2 | async-start | bytes 16384 | tf_op jit(solution)/shard_map/all_to_all | solution.py:147
  56.5 28.4 %all-to-all-start.1 = ((bf16[16,3,3,400]{3,1,2,0:T(4,128)(2,1)}), bf16[16,3,3,400]{3,1,2,0:T(4,128)(2,1)S(1)}, u32[]{:S(2)}, u32[]{:S(2)}) async-start(bf16[16,3,3,400]{3,1,2,0:T(4,128)(2,1)} %copy.78), calls=%async_computation.1 | async-start | bytes 393216 | tf_op jit(solution)/shard_map/all_to_all | solution.py:145
  60.7 2.1 collective-permute-start.2
  61.6 3.3 %collective-permute-start.3 = (bf16[2,3,1424]{2,1,0:T(4,128)(2,1)S(1)}, bf16[2,3,1424]{2,1,0:T(4,128)(2,1)S(1)}, u32[]{:S(2)}, u32[]{:S(2)}) collective-permute-start(bf16[2,3,1424]{2,1,0:T(4,128)(2,1)S(1)} %collective-permute-done.1), channel_id=1, source_target_pairs={{0,15},{1,0},{2,1},{3,2},{4,3},{5,4},{6,5},{7,6},{8,7},{9,8},{10,9... | collective-permute-start | bytes 51272 | tf_op jit(solution)/shard_map/ppermute | solution.py:23
  62.9 4.5 %collective-permute-start.4 = (bf16[2,3,1424]{2,1,0:T(4,128)(2,1)S(1)}, bf16[2,3,1424]{2,1,0:T(4,128)(2,1)S(1)}, u32[]{:S(2)}, u32[]{:S(2)}) collective-permute-start(bf16[2,3,1424]{2,1,0:T(4,128)(2,1)S(1)} %collective-permute-done.2), channel_id=1, source_target_pairs={{0,1},{1,2},{2,3},{3,4},{4,5},{5,6},{6,7},{7,8},{8,9},{9,10},{10,1... | collective-permute-start | bytes 51272 | tf_op jit(solution)/shard_map/ppermute | solution.py:20
  64.9 3.5 %collective-permute-start.5 = (bf16[2,3,1424]{2,1,0:T(4,128)(2,1)S(1)}, bf16[2,3,1424]{2,1,0:T(4,128)(2,1)S(1)}, u32[]{:S(2)}, u32[]{:S(2)}) collective-permute-start(bf16[2,3,1424]{2,1,0:T(4,128)(2,1)S(1)} %collective-permute-done.3), channel_id=1, source_target_pairs={{0,15},{1,0},{2,1},{3,2},{4,3},{5,4},{6,5},{7,6},{8,7},{9,8},{10,9... | collective-permute-start | bytes 51272 | tf_op jit(solution)/shard_map/ppermute | solution.py:23
  67.3 4.5 %collective-permute-start.6 = (bf16[2,3,1424]{2,1,0:T(4,128)(2,1)S(1)}, bf16[2,3,1424]{2,1,0:T(4,128)(2,1)S(1)}, u32[]{:S(2)}, u32[]{:S(2)}) collective-permute-start(bf16[2,3,1424]{2,1,0:T(4,128)(2,1)S(1)} %collective-permute-done.4), channel_id=1, source_target_pairs={{0,1},{1,2},{2,3},{3,4},{4,5},{5,6},{6,7},{7,8},{8,9},{9,10},{10,1... | collective-permute-start | bytes 51272 | tf_op jit(solution)/shard_map/ppermute | solution.py:20
  68.4 3.9 %collective-permute-start.7 = (bf16[2,3,1424]{2,1,0:T(4,128)(2,1)S(1)}, bf16[2,3,1424]{2,1,0:T(4,128)(2,1)S(1)}, u32[]{:S(2)}, u32[]{:S(2)}) collective-permute-start(bf16[2,3,1424]{2,1,0:T(4,128)(2,1)S(1)} %collective-permute-done.5), channel_id=1, source_target_pairs={{0,15},{1,0},{2,1},{3,2},{4,3},{5,4},{6,5},{7,6},{8,7},{9,8},{10,9... | collective-permute-start | bytes 51272 | tf_op jit(solution)/shard_map/ppermute | solution.py:23
  71.8 4.5 %collective-permute-start.8 = (bf16[2,3,1424]{2,1,0:T(4,128)(2,1)S(1)}, bf16[2,3,1424]{2,1,0:T(4,128)(2,1)S(1)}, u32[]{:S(2)}, u32[]{:S(2)}) collective-permute-start(bf16[2,3,1424]{2,1,0:T(4,128)(2,1)S(1)} %collective-permute-done.6), channel_id=1, source_target_pairs={{0,1},{1,2},{2,3},{3,4},{4,5},{5,6},{6,7},{7,8},{8,9},{9,10},{10,1... | collective-permute-start | bytes 51272 | tf_op jit(solution)/shard_map/ppermute | solution.py:20
  72.3 4.5 %collective-permute-start.9 = (bf16[2,3,1424]{2,1,0:T(4,128)(2,1)S(1)}, bf16[2,3,1424]{2,1,0:T(4,128)(2,1)S(1)}, u32[]{:S(2)}, u32[]{:S(2)}) collective-permute-start(bf16[2,3,1424]{2,1,0:T(4,128)(2,1)S(1)} %collective-permute-done.7), channel_id=1, source_target_pairs={{0,15},{1,0},{2,1},{3,2},{4,3},{5,4},{6,5},{7,6},{8,7},{9,8},{10,9... | collective-permute-start | bytes 51272 | tf_op jit(solution)/shard_map/ppermute | solution.py:23
  76.3 4.5 %collective-permute-start.10 = (bf16[2,3,1424]{2,1,0:T(4,128)(2,1)S(1)}, bf16[2,3,1424]{2,1,0:T(4,128)(2,1)S(1)}, u32[]{:S(2)}, u32[]{:S(2)}) collective-permute-start(bf16[2,3,1424]{2,1,0:T(4,128)(2,1)S(1)} %collective-permute-done.8), channel_id=1, source_target_pairs={{0,1},{1,2},{2,3},{3,4},{4,5},{5,6},{6,7},{7,8},{8,9},{9,10},{10,1... | collective-permute-start | bytes 51272 | tf_op jit(solution)/shard_map/ppermute | solution.py:20
  76.7 4.5 %collective-permute-start.11 = (bf16[2,3,1424]{2,1,0:T(4,128)(2,1)S(1)}, bf16[2,3,1424]{2,1,0:T(4,128)(2,1)S(1)}, u32[]{:S(2)}, u32[]{:S(2)}) collective-permute-start(bf16[2,3,1424]{2,1,0:T(4,128)(2,1)S(1)} %collective-permute-done.9), channel_id=1, source_target_pairs={{0,15},{1,0},{2,1},{3,2},{4,3},{5,4},{6,5},{7,6},{8,7},{9,8},{10,9... | collective-permute-start | bytes 51272 | tf_op jit(solution)/shard_map/ppermute | solution.py:23
  80.7 5.0 %collective-permute-start.12 = (bf16[2,3,1424]{2,1,0:T(4,128)(2,1)S(1)}, bf16[2,3,1424]{2,1,0:T(4,128)(2,1)S(1)}, u32[]{:S(2)}, u32[]{:S(2)}) collective-permute-start(bf16[2,3,1424]{2,1,0:T(4,128)(2,1)S(1)} %collective-permute-done.10), channel_id=1, source_target_pairs={{0,1},{1,2},{2,3},{3,4},{4,5},{5,6},{6,7},{7,8},{8,9},{9,10},{10,1... | collective-permute-start | bytes 51272 | tf_op jit(solution)/shard_map/ppermute | solution.py:20
  81.2 4.6 %collective-permute-start.13 = (bf16[2,3,1424]{2,1,0:T(4,128)(2,1)S(1)}, bf16[2,3,1424]{2,1,0:T(4,128)(2,1)S(1)}, u32[]{:S(2)}, u32[]{:S(2)}) collective-permute-start(bf16[2,3,1424]{2,1,0:T(4,128)(2,1)S(1)} %collective-permute-done.11), channel_id=1, source_target_pairs={{0,15},{1,0},{2,1},{3,2},{4,3},{5,4},{6,5},{7,6},{8,7},{9,8},{10,9... | collective-permute-start | bytes 51272 | tf_op jit(solution)/shard_map/ppermute | solution.py:23
  85.7 3.9 %collective-permute-start.14 = (bf16[2,3,1424]{2,1,0:T(4,128)(2,1)S(1)}, bf16[2,3,1424]{2,1,0:T(4,128)(2,1)S(1)}, u32[]{:S(2)}, u32[]{:S(2)}) collective-permute-start(bf16[2,3,1424]{2,1,0:T(4,128)(2,1)S(1)} %collective-permute-done.12), channel_id=1, source_target_pairs={{0,1},{1,2},{2,3},{3,4},{4,5},{5,6},{6,7},{7,8},{8,9},{9,10},{10,1... | collective-permute-start | bytes 51272 | tf_op jit(solution)/shard_map/ppermute | solution.py:20
  110.8 3.2 %slice-start = ((bf16[16,3,82048]{2,0,1:T(8,128)(2,1)}), bf16[16,3,81920]{2,0,1:T(8,128)(2,1)S(1)}, s32[]{:S(2)}) async-start(bf16[16,3,82048]{2,0,1:T(8,128)(2,1)} %tile.12), calls=%async_computation.4 | async-start | bytes 15728640 | tf_op jit(solution)/shard_map/while/body/eval_jaxpr/slice | solution.py:40
  180.7 3.2 %slice-start = ((bf16[16,3,82048]{2,0,1:T(8,128)(2,1)}), bf16[16,3,81920]{2,0,1:T(8,128)(2,1)S(1)}, s32[]{:S(2)}) async-start(bf16[16,3,82048]{2,0,1:T(8,128)(2,1)} %tile.12), calls=%async_computation.4 | async-start | bytes 15728640 | tf_op jit(solution)/shard_map/while/body/eval_jaxpr/slice | solution.py:40
  250.7 3.2 %slice-start = ((bf16[16,3,82048]{2,0,1:T(8,128)(2,1)}), bf16[16,3,81920]{2,0,1:T(8,128)(2,1)S(1)}, s32[]{:S(2)}) async-start(bf16[16,3,82048]{2,0,1:T(8,128)(2,1)} %tile.12), calls=%async_computation.4 | async-start | bytes 15728640 | tf_op jit(solution)/shard_map/while/body/eval_jaxpr/slice | solution.py:40
  301.2 14.1 %all-to-all-start.3 = ((f32[16,3,768]{2,1,0:T(4,128)}), f32[16,3,768]{2,1,0:T(4,128)S(1)}, u32[]{:S(2)}, u32[]{:S(2)}) async-start(f32[16,3,768]{2,1,0:T(4,128)} %reshape_reshape.15), calls=%async_computation.3 | async-start | bytes 393216 | tf_op jit(solution)/shard_map/all_to_all | solution.py:165
